TPU v7x, 32 devices: a whole 2x2x4 slice. The times are simulated.
32 devices in a mesh: lat: 16 (over z, y, x), field: 2 (over core).
Axes of the slice: x: 2, y: 2, z: 4, core: 2. Of those that a mesh axis runs over, the one named last changes fastest.
Arguments:
- fields_grid: bfloat16 [2, 64, 2, 48, 192], P('field', None, None, 'lat'), may hold values from -6 to 6
- basis: bfloat16 [128, 48, 96], P('lat'), may hold values from -0.875 to 0.875
- order_table: int32 [16, 8], replicated, may hold values from -1 to 95, as said below
- panel_modes: int32 [2, 64], replicated, may hold values from 0 to 95, as said below
Outputs:
- panel: bfloat16 [2, 128, 192, 128], P('field', 'lat')
Inputs may be any that keep to these rules, and one draw needn't show every extreme that they name: `order_table`: each order 0 to 95 stands in exactly one slot; every other slot holds -1; some group has all 8 slots filled. `panel_modes`: row 1 is never smaller than row 0 in the same column; degree 95 appears.
All inputs are finite; a program needn't handle non-finite values.
Results may differ from a plain program's by a relative error of at most 0.0082.
Values may be sent and summed in bfloat16 or wider, within the bound.
A program may use at most 64 MiB of HBM per device.

v0:
```python
import math
import jax
import jax.numpy as jnp
from jax import lax
from jax.sharding import PartitionSpec as P


def dft_table(orders, lon_count):
    valid_slot = orders >= 0
    safe_orders = jnp.maximum(orders, 0)
    products = lax.broadcasted_iota(jnp.int32, (lon_count, 1), 0) * safe_orders[None, :] % lon_count
    angles = products.astype(jnp.float32) * (2.0 * math.pi / lon_count)
    cosine = jnp.where(valid_slot[None, :], jnp.cos(angles), 0.0).astype(jnp.bfloat16)
    sine_table = jnp.where(valid_slot[None, :], -jnp.sin(angles), 0.0).astype(jnp.bfloat16)
    return jnp.stack([cosine, sine_table], axis=1)


def local(fields_grid, basis, order_table, panel_modes):
    grid_one = fields_grid[0]
    snap_count = grid_one.shape[0]
    pair_count = grid_one.shape[2]
    lon_count = grid_one.shape[3]
    slot_count = order_table.shape[1]
    deg_count = basis.shape[2]
    pair_total = basis.shape[1]
    mode_count = panel_modes.shape[1]
    orders = order_table.reshape(-1)
    slot_all = orders.shape[0]
    dft = dft_table(orders, lon_count)
    fourier = jnp.einsum("thjn,nrk->hkjrt", grid_one, dft, preferred_element_type=jnp.float32) * (
        1.0 / math.sqrt(lon_count)
    )
    fourier = fourier.reshape(2, slot_all, pair_count, 2 * snap_count)
    parity_parts = jnp.stack([fourier[0] + fourier[1], fourier[0] - fourier[1]]).astype(
        jnp.bfloat16
    )
    group_index = lax.axis_index("lat")
    my_orders = lax.dynamic_slice_in_dim(order_table, group_index, 1, 0)[0]
    my_odd = my_orders % 2 == 1
    basis_split = basis.reshape(slot_count, pair_total, deg_count // 2, 2)
    even_rows = basis_split[:, :, :, 0]
    odd_rows = basis_split[:, :, :, 1]
    degree = lax.broadcasted_iota(jnp.int32, (1, deg_count), 1)
    keep_mask = (degree >= my_orders[:, None]) & (my_orders >= 0)[:, None]
    received = lax.all_to_all(parity_parts, "lat", split_axis=1, concat_axis=2, tiled=True)
    first_parity = jnp.where(my_odd[:, None, None], received[1], received[0])
    second = jnp.where(my_odd[:, None, None], received[0], received[1])
    low_degrees = jnp.einsum(
        "sjh,sjc->shc", even_rows, first_parity, preferred_element_type=jnp.float32
    )
    high_degrees = jnp.einsum("sjh,sjc->shc", odd_rows, second, preferred_element_type=jnp.float32)
    joined = jnp.stack([low_degrees, high_degrees], axis=2).reshape(slot_count, deg_count, -1)
    coefficients = jnp.where(keep_mask[:, :, None], joined, 0.0).astype(jnp.bfloat16)
    mode_order = panel_modes[0]
    mode_degree = panel_modes[1]
    onehot = (my_orders[None, :] == mode_order[:, None]).astype(jnp.bfloat16)
    picked = jnp.take(coefficients, mode_degree, axis=1)
    local_values = jnp.einsum("ms,smc->mc", onehot, picked, preferred_element_type=jnp.float32)
    field_index = lax.axis_index("field")
    both_fields = jnp.stack(
        [
            jnp.where(field_index == 0, local_values, 0.0),
            jnp.where(field_index == 1, local_values, 0.0),
        ]
    )
    summed = lax.psum(both_fields, ("lat", "field"))
    other_field = jnp.where(field_index == 0, summed[1], summed[0]).astype(jnp.bfloat16)
    columns = other_field.astype(jnp.float32).reshape(mode_count * 2, snap_count)
    centered = (columns - jnp.mean(columns, axis=1, keepdims=True)).astype(jnp.bfloat16)
    coef_rows = coefficients.reshape(slot_count * deg_count * 2, snap_count)
    panel_values = lax.dot_general(
        coef_rows, centered, (((1,), (1,)), ((), ())), preferred_element_type=jnp.float32
    )
    panel_values = panel_values * (1.0 / (snap_count - 1))
    return panel_values.astype(jnp.bfloat16).reshape(1, slot_count, 2 * deg_count, 2 * mode_count)


def solution(mesh):
    placed = (P("field", None, None, "lat", None), P("lat", None, None), P(), P())
    return jax.shard_map(
        local, mesh=mesh, in_specs=placed, out_specs=P("field", "lat", None, None), check_vma=False
    )
```

profile of v0, /device:TPU:0, one launch (start us, length us, event | category | flops | bytes accessed | tf_op | source)
XLA Modules:
  0.0 63.5 jit_solution(17050038539362757233)
XLA Ops:
  0.0 0.8 %broadcast_compare_fusion = pred[16,8]{0,1:T(8,128)(4,1)S(1)} fusion(s32[16,8]{0,1:T(8,128)} %param.6), kind=kLoop, calls=%fused_computation.57 | loop fusion | flops 128 | bytes 640 | tf_op jit(solution)/shard_map/ge | solution.py:9
  0.8 0.0 copy-done.1
  0.8 0.1 copy.39
  0.9 0.1 ge.51
  1.0 0.1 copy.40
  1.0 0.1 max.11
  1.1 0.4 select_convert_fusion.1
  1.6 1.1 %fusion.1 = f32[2,128,3,2,64]{1,4,2,0,3:T(8,128)S(1)} fusion(bf16[64,2,3,192]{3,1,2,0:T(2,128)(2,1)} %bitcast.69, bf16[192,1,128]{2,0,1:T(8,128)(2,1)S(1)} %get-tuple-element.16, bf16[192,1,128]{2,0,1:T(8,128)(2,1)S(1)} %get-tuple-element.15), kind=kOutput, calls=%fused_computation.4 | convolution fusion | flops 38043648 | bytes 638976 | tf_op jit(solution)/shard_map/thjn,nrk->hkjrt/dot_general | solution.py:30
  2.8 0.8 %copy.44 = bf16[2,128,3,128]{3,0,2,1:T(2,128)(2,1)} copy(bf16[2,128,3,128]{1,3,2,0:T(8,128)(2,1)S(1)} %pad_maximum_fusion.1) | data formatting | bytes 393216 | tf_op jit(solution)/shard_map/stack | solution.py:34
  3.7 8.5 %all-to-all-start = ((bf16[2,128,3,128]{3,0,2,1:T(2,128)(2,1)}), bf16[2,128,3,128]{3,0,2,1:T(2,128)(2,1)S(1)}, u32[]{:S(2)}, u32[]{:S(2)}) async-start(bf16[2,128,3,128]{3,0,2,1:T(2,128)(2,1)} %copy.44), calls=%async_computation | async-start | bytes 393216 | tf_op jit(solution)/shard_map/all_to_all | solution.py:45
  12.1 0.0 copy-start.2
  12.2 0.7 %copy-done.2 = s32[2,64]{1,0:T(2,128)S(1)} copy-done((s32[2,64]{1,0:T(2,128)S(1)}, s32[2,64]{1,0:T(2,128)}, u32[]{:S(2)}) %copy-start.2) | copy-done | bytes 536
  12.8 0.2 dynamic-slice_reduce_fusion
  13.0 0.1 compare_bitcast_fusion
  13.2 0.2 copy.48
  13.4 7.4 %all-to-all-done = bf16[2,128,3,128]{3,0,2,1:T(2,128)(2,1)S(1)} async-done(((bf16[2,128,3,128]{3,0,2,1:T(2,128)(2,1)}), bf16[2,128,3,128]{3,0,2,1:T(2,128)(2,1)S(1)}, u32[]{:S(2)}, u32[]{:S(2)}) %all-to-all-start) | async-done | bytes 196640 | tf_op jit(solution)/shard_map/all_to_all | solution.py:45
  20.9 0.1 bitcast_select_fusion.2
  21.0 0.2 convolution_bitcast_fusion.1
  21.2 0.2 convolution_bitcast_fusion
  21.4 0.1 copy.53
  21.5 0.2 fusion.2
  21.7 0.6 gather_fusion
  22.3 0.3 fusion.5
  22.6 39.0 %psum.7 = bf16[2,64,128]{2,1,0:T(8,128)(2,1)S(1)} all-reduce(f32[2,64,128]{2,1,0:T(8,128)S(1)} %pad_maximum_fusion.2), channel_id=1, replica_groups=mesh['lat'=16,'field'=2] {'lat','field'}, use_global_device_ids=true, to_apply=%region_0.1 | all-reduce | flops 16384 | bytes 98304 | tf_op jit(solution)/shard_map/psum | solution.py:66
  61.6 0.1 reshape.345
  61.7 0.1 reduce_sum.9
  61.8 0.1 div.10
  62.0 0.1 sub.26
  62.1 0.1 sub.27
  62.2 0.1 convert_element_type.92
  62.3 0.2 convert_element_type.86
  62.5 1.0 %fusion = bf16[1536,128]{1,0:T(8,128)(2,1)} fusion(bf16[1536,64]{1,0:T(8,128)(2,1)S(1)} %convert_element_type.86, bf16[128,64]{1,0:T(8,128)(2,1)S(1)} %convert_element_type.92), kind=kOutput, calls=%fused_computation.2 | convolution fusion | flops 25559040 | bytes 606208 | tf_op jit(solution)/shard_map/dot_general | solution.py:71
  (26 shorter events, 0.3 us)
Async XLA Ops:
  0.0 0.8 %copy-start.1 = (s32[16,8]{0,1:T(8,128)S(1)}, s32[16,8]{0,1:T(8,128)}, u32[]{:S(2)}) copy-start(s32[16,8]{0,1:T(8,128)} %param.6) | copy-start | bytes 1540
  3.7 9.5 %copy-start = (bf16[8,48,96]{2,1,0:T(8,128)(2,1)S(1)}, bf16[8,48,96]{2,1,0:T(8,128)(2,1)}, u32[]{:S(2)}) copy-start(bf16[8,48,96]{2,1,0:T(8,128)(2,1)} %param.5) | copy-start | bytes 221188
  3.7 17.1 %all-to-all-start = ((bf16[2,128,3,128]{3,0,2,1:T(2,128)(2,1)}), bf16[2,128,3,128]{3,0,2,1:T(2,128)(2,1)S(1)}, u32[]{:S(2)}, u32[]{:S(2)}) async-start(bf16[2,128,3,128]{3,0,2,1:T(2,128)(2,1)} %copy.44), calls=%async_computation | async-start | bytes 393216 | tf_op jit(solution)/shard_map/all_to_all | solution.py:45
  12.1 0.7 %copy-start.2 = (s32[2,64]{1,0:T(2,128)S(1)}, s32[2,64]{1,0:T(2,128)}, u32[]{:S(2)}) copy-start(s32[2,64]{1,0:T(2,128)} %param.7) | copy-start | bytes 1540
where the time goes:
time: 63.9 us; the launch traced here: 63.5 us
  blocking collectives  39 us (61%)
  starting transfers between devices  8.47 us (13%)
  waiting for transfers between devices  7.41 us (12%)
  local copies, waits for them, and re-layouts  3.74 us (6%)
  matrix products  2.79 us (4%)
  other arithmetic  1.84 us (3%)
    psum x1, blocking collectives, local(): summed = lax.psum(both_fields, ('lat', 'field'))  39 us
    all_to_all x1, starting transfers between devices, local(): lax.all_to_all(parity_parts, 'lat', split_axis=1, concat_axis=2, tiled=True)  8.47 us
    all_to_all x1, waiting for transfers between devices, local(): lax.all_to_all(parity_parts, 'lat', split_axis=1, concat_axis=2, tiled=True)  7.41 us
  transfers between devices with their start and end apart: 1, of which 1 were waited for; matrix products, arithmetic and copies ran while one was open for 1% of the time, Pallas kernels for 0%

commit v1 on v0

--- a/solution.py
+++ b/solution.py
@@ -63,7 +63,7 @@
             jnp.where(field_index == 1, local_values, 0.0),
         ]
     )
-    summed = lax.psum(both_fields, ("lat", "field"))
+    summed = lax.psum(lax.psum(both_fields, "field"), "lat")
     other_field = jnp.where(field_index == 0, summed[1], summed[0]).astype(jnp.bfloat16)
     columns = other_field.astype(jnp.float32).reshape(mode_count * 2, snap_count)
     centered = (columns - jnp.mean(columns, axis=1, keepdims=True)).astype(jnp.bfloat16)

time: 63.9 us -> 132 us (2.07)
  blocking collectives: 39 us -> 77.7 us
  waiting for transfers between devices: 7.41 us -> 22.8 us
  between operations: 0.28 us -> 13.6 us
    psum x1, blocking collectives: 39 us -> 77.7 us  [local(): summed = lax.psum(lax.psum(both_fields, 'field'), 'lat')]
    psum x0 -> x1, waiting for transfers between devices: none -> 15.4 us  [local(): summed = lax.psum(lax.psum(both_fields, 'field'), 'lat')]
  transfers between devices with their start and end apart: 1 -> 2, of which waited for: 1 -> 2; matrix products, arithmetic and copies ran while one was open for 1% -> 1% of each run, Pallas kernels for 0% -> 0%
where the time goes in v1:
time: 132 us
  blocking collectives  77.7 us (59%)
  waiting for transfers between devices  22.8 us (17%)
  between operations  13.6 us (10%)
  starting transfers between devices  8.51 us (6%)
  local copies, waits for them, and re-layouts  3.7 us (3%)
  matrix products  2.79 us (2%)
  other arithmetic  2.48 us (2%)
    psum x1, blocking collectives, local(): summed = lax.psum(lax.psum(both_fields, 'field'), 'lat')  77.7 us
    psum x1, waiting for transfers between devices, local(): summed = lax.psum(lax.psum(both_fields, 'field'), 'lat')  15.4 us
    all_to_all x1, starting transfers between devices, local(): lax.all_to_all(parity_parts, 'lat', split_axis=1, concat_axis=2, tiled=True)  8.47 us
    all_to_all x1, waiting for transfers between devices, local(): lax.all_to_all(parity_parts, 'lat', split_axis=1, concat_axis=2, tiled=True)  7.41 us
  transfers between devices with their start and end apart: 2, of which 2 were waited for; matrix products, arithmetic and copies ran while one was open for 1% of the time, Pallas kernels for 0%

profile of v1, /device:TPU:0, one launch (start us, length us, event | category | flops | bytes accessed | tf_op | source)
XLA Modules:
  0.0 131.7 jit_solution(16327015163990602540)
XLA Ops:
  6.5 0.8 broadcast_compare_fusion
  7.3 0.1 copy.39
  7.4 0.1 ge.51
  7.5 0.1 copy.40
  7.6 0.1 max.11
  7.7 0.4 select_convert_fusion.1
  8.1 1.1 fusion.1
  9.3 0.8 copy.44
  10.2 8.5 %all-to-all-start = ((bf16[2,128,3,128]{3,0,2,1:T(2,128)(2,1)}), bf16[2,128,3,128]{3,0,2,1:T(2,128)(2,1)S(1)}, u32[]{:S(2)}, u32[]{:S(2)}) async-start(bf16[2,128,3,128]{3,0,2,1:T(2,128)(2,1)} %copy.44), calls=%async_computation | async-start | bytes 393216 | tf_op jit(solution)/shard_map/all_to_all | solution.py:45
  18.7 0.6 copy-done.2
  19.4 0.2 dynamic-slice_reduce_fusion
  19.6 0.1 compare_bitcast_fusion
  19.7 0.2 copy.48
  19.9 7.4 %all-to-all-done = bf16[2,128,3,128]{3,0,2,1:T(2,128)(2,1)S(1)} async-done(((bf16[2,128,3,128]{3,0,2,1:T(2,128)(2,1)}), bf16[2,128,3,128]{3,0,2,1:T(2,128)(2,1)S(1)}, u32[]{:S(2)}, u32[]{:S(2)}) %all-to-all-start) | async-done | bytes 196640 | tf_op jit(solution)/shard_map/all_to_all | solution.py:45
  27.4 0.1 bitcast_select_fusion.2
  27.5 0.2 convolution_bitcast_fusion.1
  27.7 0.2 convolution_bitcast_fusion
  27.9 0.1 copy.53
  28.0 0.2 fusion.2
  28.2 0.6 gather_fusion
  28.8 0.3 fusion.5
  29.1 0.6 pad_maximum_fusion.2
  29.8 0.2 convert_element_type.86
  30.0 15.4 %all-reduce.2.cloned.1.call-done = f32[2,64,128]{2,1,0:T(8,128)} async-done(((f32[2,64,128]{2,1,0:T(8,128)}), f32[2,64,128]{2,1,0:T(8,128)}) %all-reduce.2.cloned.1.call-update) | async-done | bytes 65552 | tf_op jit(solution)/shard_map/psum | solution.py:66
  45.4 77.7 %psum.15 = bf16[2,64,128]{2,1,0:T(8,128)(2,1)S(1)} all-reduce(f32[2,64,128]{2,1,0:T(8,128)} %all-reduce.2.cloned.1.call-done), channel_id=1, replica_groups=mesh['lat'=16,'field'=2] {'lat'}, use_global_device_ids=true, to_apply=%region_1.2 | all-reduce | flops 16384 | bytes 98304 | tf_op jit(solution)/shard_map/psum | solution.py:66
  123.1 0.1 reshape.345
  123.2 0.1 reduce_sum.9
  123.3 0.1 div.10
  123.5 0.1 sub.26
  123.6 0.1 sub.27
  123.7 0.1 convert_element_type.92
  123.8 1.0 fusion
  (29 shorter events, 0.4 us)
Async XLA Ops:
  6.5 0.8 copy-start.1
  10.2 9.5 %copy-start = (bf16[8,48,96]{2,1,0:T(8,128)(2,1)S(1)}, bf16[8,48,96]{2,1,0:T(8,128)(2,1)}, u32[]{:S(2)}) copy-start(bf16[8,48,96]{2,1,0:T(8,128)(2,1)} %param.5) | copy-start | bytes 221188
  10.2 17.1 %all-to-all-start = ((bf16[2,128,3,128]{3,0,2,1:T(2,128)(2,1)}), bf16[2,128,3,128]{3,0,2,1:T(2,128)(2,1)S(1)}, u32[]{:S(2)}, u32[]{:S(2)}) async-start(bf16[2,128,3,128]{3,0,2,1:T(2,128)(2,1)} %copy.44), calls=%async_computation | async-start | bytes 393216 | tf_op jit(solution)/shard_map/all_to_all | solution.py:45
  18.7 0.7 copy-start.2
  18.7 26.7 %all-reduce.2.cloned.1.call-start = ((), (), s32[]{:S(2)}) async-start(), calls=%async_computation.1 | async-start | bytes 131072 | tf_op jit(solution)/shard_map/psum | solution.py:66
Sparse Core Ops, SparseCore 0:
  29.9 15.4 all-reduce.1
